TPU v7x, 32 devices: a whole 2x2x4 slice. The times are simulated.
32 devices in a mesh: segment: 2 (over core), clip: 4 (over z), tile: 4 (over y, x).
Axes of the slice: x: 2, y: 2, z: 4, core: 2. Of those that a mesh axis runs over, the one named last changes fastest.
Arguments:
- video: bfloat16 [4, 4, 3, 12, 4, 256], P('clip', 'tile'), may hold values from -6 to 6
- cotangent: bfloat16 [4, 4, 3, 12, 4, 256], P('clip', 'tile'), may hold values from -6 to 6
- weights: bfloat16 [2, 27, 256, 256], P('segment'), may hold values from -0.078125 to 0.078125
- neighbours: int32 [4, 4, 2], P('clip', 'tile'), may hold values from 0 to 4, as said below
- rows_used: int32 [4, 4], P('clip', 'tile'), may hold values from 3 to 12, as said below
- cols_used: int32 [4], P('clip'), may hold values from 2 to 4, as said below
Outputs:
- section_out: bfloat16 [2, 4, 4, 3, 12, 4, 256], P('segment', 'clip', 'tile')
- grads: float32 [2, 3, 589824], P('segment', None, ('clip', 'tile'))
Inputs may be any that keep to these rules, and one draw needn't show every extreme that they name: `neighbours`: in each clip the strips of its frames lie on the 4 tiles in an order of their own: entry 0 names the tile of the strip above, entry 1 the tile of the strip below, 4 where there is none; exactly one strip of each clip has none above and one has none below, and the entries chain all 4 strips of a clip top to bottom. `rows_used`: in every clip some strip has 12 rows. `cols_used`: some clip has 4 columns.
All inputs are finite; a program needn't handle non-finite values.
Results may differ from a plain program's by a relative error of at most 0.0054.
Values may be sent and summed in bfloat16 or wider, within the bound.
A program may use at most 576 MiB of HBM per device.

v0:
```python
import jax
import jax.numpy as jnp
from jax import lax
from jax.sharding import PartitionSpec as P


def shifted(block, axis, distance):
    devices = range(lax.axis_size(axis))
    route = [(i - distance, i) for i in devices if i - distance in devices]
    return lax.ppermute(block, axis, route)


def silu_grad(values):
    sigmoid = jax.nn.sigmoid(values)
    return sigmoid * (1.0 + values * (1.0 - sigmoid))


def pad_block(strip_field, upper, bottom, row_count):
    frame_count, height, columns, channels = strip_field.shape
    blank = jnp.zeros((frame_count, 1, columns, channels), strip_field.dtype)
    padded = jnp.concatenate([upper[:, None], strip_field, blank], axis=1)
    padded = lax.dynamic_update_slice_in_dim(padded, bottom[:, None], row_count + 1, axis=1)
    return jnp.pad(padded, ((0, 0), (0, 0), (1, 1), (0, 0)))


def patches(stacked, frame_count, height, columns):
    pieces = []
    for depth_off in range(3):
        for row_off in range(3):
            for col_off in range(3):
                pieces.append(
                    stacked[
                        depth_off : depth_off + frame_count,
                        row_off : row_off + height,
                        col_off : col_off + columns,
                    ]
                )
    return jnp.concatenate(pieces, axis=-1).reshape(frame_count * height * columns, -1)


def own_entries(padded, weighting, axes):
    frame_count, tall, columns, channels = padded.shape
    height = tall - 2
    payload = jnp.concatenate([padded.reshape(-1, channels), weighting], axis=0)
    gathered = lax.all_gather(payload, axes, axis=0)
    cut = frame_count * tall * columns
    strips = gathered[:, :cut].reshape(-1, frame_count, tall, columns, channels)
    strips = jnp.pad(strips, ((0, 0), (2, 0), (0, 0), (1, 1), (0, 0)))
    upstream = gathered[:, cut:].reshape(-1, channels)
    row_total = 9 * channels // lax.axis_size(axes)
    start = lax.axis_index(axes) * row_total
    low = jnp.minimum(start // channels, 8)
    lower = []
    for step in range(-(-row_total // channels) + 1):
        tap = jnp.minimum(low + step, 8)
        lower.append(
            lax.dynamic_slice(
                strips,
                (0, 0, tap // 3, tap % 3, 0),
                (strips.shape[0], frame_count + 2, height, columns, channels),
            )
        )
    window = jnp.concatenate(lower, axis=-1)
    window = lax.dynamic_slice_in_dim(window, start - low * channels, row_total, 4)
    contract = (((0,), (0,)), ((), ()))
    return jnp.stack(
        [
            lax.dot_general(
                window[:, tap : tap + frame_count].reshape(-1, row_total),
                upstream,
                contract,
                preferred_element_type=jnp.float32,
            ).reshape(-1)
            for tap in range(3)
        ]
    )


def local(video, cotangent, weights, neighbours, rows_used, cols_used):
    window = video[0, 0]
    frame_count, height, columns, channels = window.shape
    tile_count = lax.axis_size("tile")
    section = lax.axis_index("segment")
    row_count = rows_used[0, 0]
    col_count = cols_used[0]
    upper_tile = neighbours[0, 0, 0]
    lower_tile = neighbours[0, 0, 1]
    row_ids = jnp.arange(height, dtype=jnp.int32)
    col_ids = jnp.arange(columns, dtype=jnp.int32)
    inside = (row_ids[:, None] < row_count) & (col_ids[None, :] < col_count)
    inside_mask = inside[None, :, :, None]
    kernel = weights[0]
    forward_mat = kernel.reshape(27 * channels, channels)
    backward_mat = kernel[::-1].transpose(0, 2, 1).reshape(27 * channels, channels)
    front_zero = jnp.zeros((2, height + 2, columns + 2, channels), jnp.bfloat16)

    def halo_block(field):
        leading = field[:, 0]
        trailing = lax.dynamic_index_in_dim(field, row_count - 1, axis=1, keepdims=False)
        both_rows = jnp.stack([leading, trailing], axis=1)
        gathered = lax.all_gather(both_rows[None], "tile", axis=0, tiled=True)
        upper = gathered[jnp.minimum(upper_tile, tile_count - 1), :, 1]
        bottom = gathered[jnp.minimum(lower_tile, tile_count - 1), :, 0]
        upper = jnp.where(upper_tile < tile_count, upper, jnp.zeros_like(upper))
        bottom = jnp.where(lower_tile < tile_count, bottom, jnp.zeros_like(bottom))
        return pad_block(field, upper, bottom, row_count)

    def advance(entry, history):
        count = entry.shape[0]
        activated = jax.nn.silu(entry.astype(jnp.float32)).astype(jnp.bfloat16)
        padded = halo_block(activated)
        stacked = jnp.concatenate([history, padded], axis=0)
        mixed = jnp.dot(
            patches(stacked, count, height, columns),
            forward_mat,
            preferred_element_type=jnp.float32,
        ).reshape(entry.shape)
        result = jnp.where(inside_mask, entry.astype(jnp.float32) + mixed, 0.0).astype(jnp.bfloat16)
        return (result, stacked[-2:], padded)

    source = jnp.where(inside_mask, window, jnp.zeros_like(window))
    is_encoder = section == 0
    first_out, first_hist, first_pad = advance(source, front_zero)
    latent = shifted(first_out, "segment", 1)
    second_out, second_hist, second_pad = advance(latent, front_zero)
    own_out = jnp.where(is_encoder, first_out, second_out)
    own_input = jnp.where(is_encoder, source, latent)
    own_pad = jnp.where(is_encoder, first_pad, second_pad)
    target = jnp.where(inside_mask, cotangent[0, 0], jnp.zeros_like(cotangent[0, 0]))
    back_stack = jnp.concatenate([halo_block(target), front_zero], axis=0)
    spread = jnp.dot(
        patches(back_stack, frame_count, height, columns),
        backward_mat,
        preferred_element_type=jnp.float32,
    ).reshape(target.shape)
    own_grad = jnp.where(
        inside_mask,
        target.astype(jnp.float32) + silu_grad(own_input.astype(jnp.float32)) * spread,
        0.0,
    ).astype(jnp.bfloat16)
    returned = shifted(own_grad, "segment", -1)
    weighting = jnp.where(is_encoder, returned, target).reshape(-1, channels)
    summed = own_entries(own_pad[:, :, 1:-1], weighting, ("clip", "tile"))
    return (own_out[None, None, None], summed[None])


def solution(mesh):
    in_specs = (
        P("clip", "tile", None, None, None, None),
        P("clip", "tile", None, None, None, None),
        P("segment", None, None, None),
        P("clip", "tile", None),
        P("clip", "tile"),
        P("clip"),
    )
    out_specs = (
        P("segment", "clip", "tile", None, None, None, None),
        P("segment", None, ("clip", "tile")),
    )
    return jax.shard_map(local, mesh=mesh, in_specs=in_specs, out_specs=out_specs, check_vma=False)
```

profile of v0, /device:TPU:0, one launch (start us, length us, event | category | flops | bytes accessed | tf_op | source)
XLA Modules:
  0.0 162.4 jit_solution(4665979440617564632)
XLA Ops:
  7.2 1.3 fusion.28
  12.5 1.0 bitcast_select_fusion
  13.5 1.0 fusion.19
  14.6 9.7 %all-gather = bf16[12,2,4,256]{3,2,1,0:T(4,128)(2,1)S(1)} all-gather(bf16[3,2,4,256]{3,2,1,0:T(4,128)(2,1)S(1)} %copy.132), channel_id=2, replica_groups=mesh['segment'=2,'clip'=4,'tile'=4] {'tile'}, dimensions={0}, use_global_device_ids=true | all-gather | bytes 61440 | tf_op jit(solution)/shard_map/all_gather | solution.py:101
  24.4 8.2 %all-gather.2 = bf16[12,2,4,256]{3,2,1,0:T(4,128)(2,1)S(1)} all-gather(bf16[3,2,4,256]{3,2,1,0:T(4,128)(2,1)S(1)} %copy.140), channel_id=4, replica_groups=mesh['segment'=2,'clip'=4,'tile'=4] {'tile'}, dimensions={0}, use_global_device_ids=true | all-gather | bytes 61440 | tf_op jit(solution)/shard_map/all_gather | solution.py:101
  33.7 1.4 copy-done
  35.0 0.9 fusion.3
  35.9 1.3 collective-permute-start
  37.3 5.8 %copy.143 = bf16[1,27,256,256]{2,3,1,0:T(8,128)(2,1)} copy(bf16[1,27,256,256]{3,2,1,0:T(8,128)(2,1)} %param.8) | data formatting | bytes 7077888 | tf_op args[2]
  43.7 4.2 %rev.3 = bf16[27,256,256]{1,2,0:T(8,128)(2,1)} reverse(bf16[27,256,256]{1,2,0:T(8,128)(2,1)} %bitcast.88), dimensions={0} | reverse | bytes 7077888 | tf_op jit(solution)/shard_map/rev | solution.py:94
  48.0 3.0 %fusion.15 = (bf16[3,12,4,256]{3,1,2,0:T(8,128)(2,1)S(1)}, bf16[3,12,4,256]{3,1,2,0:T(8,128)(2,1)S(1)}) fusion(bf16[3,12,4,256]{3,1,2,0:T(8,128)(2,1)S(1)} %collective-permute-done, pred[12,4]{0,1:T(4,128)(4,1)S(1)} %broadcast_and_fusion, pred[]{:T(512)S(6)} %eq.6, bf16[1,1,3,12,4,256]{5,4,3,2,1,0:T(4,128)(2,1)S(1)} %copy-done.5, ...), kind=kOutput, calls=%fused_computation.85 | convolution fusion | flops 510418944 | bytes 5898289 | tf_op jit(solution)/shard_map/dot_general | solution.py:131
  51.0 7.3 %all-gather.1 = bf16[12,2,4,256]{3,2,1,0:T(4,128)(2,1)S(1)} all-gather(bf16[3,2,4,256]{3,2,1,0:T(4,128)(2,1)S(1)} %copy.135), channel_id=3, replica_groups=mesh['segment'=2,'clip'=4,'tile'=4] {'tile'}, dimensions={0}, use_global_device_ids=true | all-gather | bytes 61440 | tf_op jit(solution)/shard_map/all_gather | solution.py:101
  58.5 1.3 collective-permute-start.1
  59.9 1.7 %collective-permute-done.1 = bf16[3,12,4,256]{3,1,2,0:T(8,128)(2,1)S(1)} collective-permute-done((bf16[3,12,4,256]{3,1,2,0:T(8,128)(2,1)S(1)}, bf16[3,12,4,256]{3,1,2,0:T(8,128)(2,1)S(1)}, u32[]{:S(2)}, u32[]{:S(2)}) %collective-permute-start.1) | collective-permute-done | bytes 73760 | tf_op jit(solution)/shard_map/ppermute | solution.py:10
  61.8 0.7 pad_maximum_fusion.1
  63.3 1.4 copy-done.1
  64.7 0.9 fusion.6
  66.3 60.1 %all-gather.6.cloned.1.call-done = bf16[4992,256]{1,0:T(8,128)(2,1)} async-done(((bf16[312,256]{1,0:T(8,128)(2,1)}), bf16[4992,256]{1,0:T(8,128)(2,1)}) %all-gather.6.cloned.1.call-update) | async-done | bytes 2555920 | tf_op jit(solution)/shard_map/all_gather | solution.py:45
  126.4 2.5 %slice.389 = bf16[16,168,256]{2,1,0:T(8,128)(2,1)} slice(bf16[16,312,256]{2,1,0:T(8,128)(2,1)} %bitcast.90), slice={[0:16], [0:168], [0:256]} | slice | bytes 2752512 | tf_op jit(solution)/shard_map/slice | solution.py:47
  128.9 1.3 slice.391
  130.2 2.9 %reshape.170 = bf16[16,3,14,4,256]{4,3,2,1,0:T(4,128)(2,1)S(1)} reshape(bf16[16,168,256]{2,1,0:T(8,128)(2,1)} %slice.389) | data formatting | bytes 2752512 | tf_op jit(solution)/shard_map/reshape | solution.py:47
  133.1 3.5 %pad_dynamic-slice_fusion = (bf16[16,5,12,4,256]{4,3,2,1,0:T(4,128)(2,1)S(1)}, bf16[16,5,12,4,256]{4,3,2,1,0:T(4,128)(2,1)S(1)}) fusion(s32[]{:T(128)S(6)} %select_n.223, s32[]{:T(128)S(6)} %select_n.225, bf16[16,3,14,4,256]{4,3,2,1,0:T(4,128)(2,1)S(1)} %reshape.170, s32[]{:T(128)S(6)} %select_n.219, s32[]{:T(128)S(6)} %select_n.221), kind=kLoop, calls=%fused_computation | loop fusion | bytes 5308432 | tf_op jit(solution)/shard_map/dynamic_slice | solution.py:57
  136.6 3.8 %fusion = bf16[16,5,12,4,144]{4,3,2,1,0:T(4,128)(2,1)S(1)} fusion(s32[]{:T(128)S(6)} %select_n.226, bf16[16,5,12,4,256]{4,3,2,1,0:T(4,128)(2,1)S(1)} %get-tuple-element.22, bf16[16,5,12,4,256]{4,3,2,1,0:T(4,128)(2,1)S(1)} %get-tuple-element.21), kind=kLoop, calls=%fused_computation.4 | loop fusion | flops 2211840 | bytes 5038084 | tf_op jit(solution)/shard_map/concatenate | solution.py:63
  140.4 2.1 %fusion.24 = (bf16[16,3,12,4,144]{4,3,2,1,0:T(4,128)(2,1)}, bf16[16,3,12,4,144]{4,3,2,1,0:T(4,128)(2,1)S(1)}, bf16[16,3,12,4,144]{4,3,2,1,0:T(4,128)(2,1)S(1)}) fusion(bf16[16,5,12,4,144]{4,3,2,1,0:T(4,128)(2,1)S(1)} %fusion), kind=kLoop, calls=%fused_computation.198 | loop fusion | bytes 3981312 | tf_op jit(solution)/shard_map/slice | solution.py:69
  142.5 3.2 %reshape.171 = bf16[2304,144]{1,0:T(8,128)(2,1)} reshape(bf16[16,3,12,4,144]{4,3,2,1,0:T(4,128)(2,1)} %get-tuple-element.18) | data formatting | bytes 1327104 | tf_op jit(solution)/shard_map/reshape | solution.py:69
  145.7 1.7 %convolution_bitcast_fusion.2 = f32[1,1,144,256]{3,2,1,0:T(8,128)S(1)} fusion(bf16[2304,144]{1,0:T(8,128)(2,1)} %reshape.171, bf16[2304,256]{1,0:T(8,128)(2,1)S(1)} %bitcast.83), kind=kOutput, calls=%fused_computation.11 | convolution fusion | flops 169869312 | bytes 1990656 | tf_op jit(solution)/shard_map/dot_general | solution.py:68
  147.4 0.8 copy.148
  148.2 1.6 reshape.173
  149.8 1.7 %convolution_bitcast_fusion.1 = f32[1,1,144,256]{3,2,1,0:T(8,128)S(1)} fusion(bf16[2304,144]{1,0:T(8,128)(2,1)} %reshape.173, bf16[2304,256]{1,0:T(8,128)(2,1)S(1)} %bitcast.84), kind=kOutput, calls=%fused_computation.10 | convolution fusion | flops 169869312 | bytes 1990656 | tf_op jit(solution)/shard_map/dot_general | solution.py:68
  151.6 0.8 copy.149
  152.4 0.7 reshape.174
  154.5 1.1 broadcast_in_dim.60
  (133 shorter events, 4.6 us)
Async XLA Ops:
  7.2 119.2 %all-gather.6.cloned.1.call-start = ((), (), s32[]{:S(2)}) async-start(), calls=%async_computation | async-start | bytes 2715648 | tf_op jit(solution)/shard_map/all_gather | solution.py:45
  33.0 2.0 %copy-start = (bf16[1,27,256,256]{3,2,1,0:T(8,128)(2,1)S(1)}, bf16[1,27,256,256]{3,2,1,0:T(8,128)(2,1)}, u32[]{:S(2)}) copy-start(bf16[1,27,256,256]{3,2,1,0:T(8,128)(2,1)} %param.8) | copy-start | bytes 10616836
  33.0 2.0 %copy-start.5 = (bf16[1,1,3,12,4,256]{5,4,3,2,1,0:T(4,128)(2,1)S(1)}, bf16[1,1,3,12,4,256]{5,4,3,2,1,0:T(4,128)(2,1)}, u32[]{:S(2)}) copy-start(bf16[1,1,3,12,4,256]{5,4,3,2,1,0:T(4,128)(2,1)} %param.6) | copy-start | bytes 221188
  35.9 12.1 %collective-permute-start = (bf16[3,12,4,256]{3,1,2,0:T(8,128)(2,1)S(1)}, bf16[3,12,4,256]{3,1,2,0:T(8,128)(2,1)S(1)}, u32[]{:S(2)}, u32[]{:S(2)}) collective-permute-start(bf16[3,12,4,256]{3,1,2,0:T(8,128)(2,1)S(1)} %fusion.3), channel_id=1, source_target_pairs={{0,16},{1,17},{2,18},{3,19},{4,20},{5,21},{6,22},{7,23},{8,24},{9,... | collective-permute-start | bytes 221192 | tf_op jit(solution)/shard_map/ppermute | solution.py:10
  43.7 4.3 %copy-start.4 = (bf16[1,1,3,12,4,256]{5,4,3,2,1,0:T(4,128)(2,1)S(1)}, bf16[1,1,3,12,4,256]{5,4,3,2,1,0:T(4,128)(2,1)}, u32[]{:S(2)}) copy-start(bf16[1,1,3,12,4,256]{5,4,3,2,1,0:T(4,128)(2,1)} %param.7) | copy-start | bytes 221188
  58.5 3.2 %collective-permute-start.1 = (bf16[3,12,4,256]{3,1,2,0:T(8,128)(2,1)S(1)}, bf16[3,12,4,256]{3,1,2,0:T(8,128)(2,1)S(1)}, u32[]{:S(2)}, u32[]{:S(2)}) collective-permute-start(bf16[3,12,4,256]{3,1,2,0:T(8,128)(2,1)S(1)} %get-tuple-element.23), channel_id=1, source_target_pairs={{16,0},{17,1},{18,2},{19,3},{20,4},{21,5},{22,6},{23,7},{24,8},{25... | collective-permute-start | bytes 221192 | tf_op jit(solution)/shard_map/ppermute | solution.py:10
  62.7 2.0 %copy-start.1 = (bf16[1,27,256,256]{3,2,1,0:T(8,128)(2,1)S(1)}, bf16[1,27,256,256]{3,2,1,0:T(8,128)(2,1)}, u32[]{:S(2)}) copy-start(bf16[1,27,256,256]{3,2,1,0:T(8,128)(2,1)} %param.8) | copy-start | bytes 10616836
  153.1 0.9 copy-start.2
  153.1 1.0 copy-start.3
Sparse Core Ops, SparseCore 0:
  62.6 63.7 all-gather.5
where the time goes:
time: 163 us; the launch traced here: 162 us
  waiting for transfers between devices  61.8 us (38%)
  local copies, waits for them, and re-layouts  37.7 us (23%)
  blocking collectives  25.2 us (15%)
  between operations  19.1 us (12%)
  matrix products  8.63 us (5%)
  other arithmetic  7.39 us (5%)
  starting transfers between devices  2.62 us (2%)
    all_gather x1, waiting for transfers between devices, own_entries(): gathered = lax.all_gather(payload, axes, axis=0)  60.1 us
    all_gather x3, blocking collectives, halo_block(): gathered = lax.all_gather(both_rows[None], 'tile', axis=0, tiled=True)  25.2 us
    unnamed x95, local copies, waits for them, and re-layouts  12.6 us
    reshape x3, local copies, waits for them, and re-layouts, own_entries(): window[:, tap:tap + frame_count].reshape(-1, row_total)  5.48 us
    rev x1, local copies, waits for them, and re-layouts, local(): kernel[::-1].transpose(0, 2, 1).reshape(27 * channels, channels)  4.22 us
    dot_general x3, matrix products, own_entries(): lax.dot_general(window[:, tap:tap + frame_count].reshape(-1, row_total),...  3.94 us
    concatenate x1, other arithmetic, own_entries(): window = jnp.concatenate(lower, axis=-1)  3.82 us
    dynamic_slice x1, local copies, waits for them, and re-layouts, own_entries(): lax.dynamic_slice(strips, (0, 0, tap // 3, tap % 3, 0), (strips.shape[0],...  3.48 us
  transfers between devices with their start and end apart: 3, of which 2 were waited for; matrix products, arithmetic and copies ran while one was open for 8% of the time, Pallas kernels for 0%

commit v1 on v0

--- a/solution.py
+++ b/solution.py
@@ -2,6 +2,18 @@
 import jax.numpy as jnp
 from jax import lax
 from jax.sharding import PartitionSpec as P
+
+
+def doubled_up(x, axis, dim):
+    ways, here = (lax.axis_size(axis), lax.axis_index(axis))
+    grown, reach = (x, 1)
+    while reach < ways:
+        theirs = lax.ppermute(grown, axis, [(d, d ^ reach) for d in range(ways)])
+        mine_first = jnp.concatenate([grown, theirs], axis=dim)
+        theirs_first = jnp.concatenate([theirs, grown], axis=dim)
+        grown = jnp.where(here & reach == 0, mine_first, theirs_first)
+        reach = 2 * reach
+    return grown
 
 
 def shifted(block, axis, distance):
@@ -98,7 +110,7 @@
         leading = field[:, 0]
         trailing = lax.dynamic_index_in_dim(field, row_count - 1, axis=1, keepdims=False)
         both_rows = jnp.stack([leading, trailing], axis=1)
-        gathered = lax.all_gather(both_rows[None], "tile", axis=0, tiled=True)
+        gathered = doubled_up(both_rows[None], "tile", 0)
         upper = gathered[jnp.minimum(upper_tile, tile_count - 1), :, 1]
         bottom = gathered[jnp.minimum(lower_tile, tile_count - 1), :, 0]
         upper = jnp.where(upper_tile < tile_count, upper, jnp.zeros_like(upper))

time: 163 us -> 152 us (0.933)
  blocking collectives: 25.2 us -> 0 us
  waiting for transfers between devices: 61.8 us -> 69.8 us
  starting transfers between devices: 2.62 us -> 9.62 us
  other arithmetic: 7.39 us -> 11.1 us
  local copies, waits for them, and re-layouts: 37.7 us -> 35.3 us
  matrix products: 8.63 us -> 6.67 us
    all_gather x3 -> x0, blocking collectives: 25.2 us -> none  [halo_block(): gathered = lax.all_gather(both_rows[None], 'tile', axis=0, tiled=True)]
    ppermute x0 -> x6, waiting for transfers between devices: none -> 8.41 us  [doubled_up(): theirs = lax.ppermute(grown, axis, [(d, d ^ reach) for d in range(ways)])]
    ppermute x0 -> x6, starting transfers between devices: none -> 6.87 us  [doubled_up(): theirs = lax.ppermute(grown, axis, [(d, d ^ reach) for d in range(ways)])]
    rev x1, local copies, waits for them, and re-layouts: 4.22 us -> 1.98 us  [local(): kernel[::-1].transpose(0, 2, 1).reshape(27 * channels, channels)]
    select_n x0 -> x6, other arithmetic: none -> 2.06 us  [doubled_up(): grown = jnp.where(here & reach == 0, mine_first, theirs_first)]
    dot_general x1, matrix products: 2.96 us -> 0.97 us  [local(): jnp.dot(patches(back_stack, frame_count, height, columns), backward_mat,...]
    unnamed x95 -> x101, local copies, waits for them, and re-layouts: 12.6 us -> 12.6 us
  transfers between devices with their start and end apart: 3 -> 9, of which waited for: 2 -> 6; matrix products, arithmetic and copies ran while one was open for 8% -> 9% of each run, Pallas kernels for 0% -> 0%
where the time goes in v1:
time: 152 us; the launch traced here: 151 us
  waiting for transfers between devices  69.8 us (46%)
  local copies, waits for them, and re-layouts  35.3 us (23%)
  between operations  18.9 us (12%)
  other arithmetic  11.1 us (7%)
  starting transfers between devices  9.62 us (6%)
  matrix products  6.67 us (4%)
    all_gather x1, waiting for transfers between devices, own_entries(): gathered = lax.all_gather(payload, axes, axis=0)  60.5 us
    unnamed x101, local copies, waits for them, and re-layouts  12.6 us
    ppermute x6, waiting for transfers between devices, doubled_up(): theirs = lax.ppermute(grown, axis, [(d, d ^ reach) for d in range(ways)])  8.41 us
    ppermute x6, starting transfers between devices, doubled_up(): theirs = lax.ppermute(grown, axis, [(d, d ^ reach) for d in range(ways)])  6.87 us
    reshape x3, local copies, waits for them, and re-layouts, own_entries(): window[:, tap:tap + frame_count].reshape(-1, row_total)  5.46 us
    dot_general x3, matrix products, own_entries(): lax.dot_general(window[:, tap:tap + frame_count].reshape(-1, row_total),...  3.94 us
    concatenate x1, other arithmetic, own_entries(): window = jnp.concatenate(lower, axis=-1)  3.82 us
    dynamic_slice x1, local copies, waits for them, and re-layouts, own_entries(): lax.dynamic_slice(strips, (0, 0, tap // 3, tap % 3, 0), (strips.shape[0],...  3.48 us
  transfers between devices with their start and end apart: 9, of which 6 were waited for; matrix products, arithmetic and copies ran while one was open for 9% of the time, Pallas kernels for 0%

profile of v1, /device:TPU:0, one launch (start us, length us, event | category | flops | bytes accessed | tf_op | source)
XLA Modules:
  0.0 151.4 jit_solution(3532956533293618021)
XLA Ops:
  8.6 1.0 bitcast_select_fusion
  10.3 3.0 %collective-permute-start.5 = (bf16[1,3,2,4,256]{4,2,3,1,0:T(2,128)(2,1)S(1)}, bf16[1,3,2,4,256]{4,2,3,1,0:T(2,128)(2,1)}, u32[]{:S(2)}, u32[]{:S(2)}) collective-permute-start(bf16[1,3,2,4,256]{4,2,3,1,0:T(2,128)(2,1)S(1)} %maximum_bitcast_fusion.2), channel_id=1, source_target_pairs={{0,1},{1,0},{2,3},{3,2},{4,5},{5,4},{6,7},{7,6},{8,9},{9,8},{10,11... | collective-permute-start | bytes 36872 | tf_op jit(solution)/shard_map/ppermute | solution.py:11
  13.3 1.0 fusion.19
  15.6 1.3 fusion.34
  19.5 4.4 %copy.41 = bf16[1,27,256,256]{2,3,1,0:T(8,128)(2,1)S(1)} copy(bf16[1,27,256,256]{3,2,1,0:T(8,128)(2,1)} %param.8) | data formatting | bytes 7077888 | tf_op args[2]
  24.0 2.0 %rev.3 = bf16[27,256,256]{1,2,0:T(8,128)(2,1)} reverse(bf16[27,256,256]{1,2,0:T(8,128)(2,1)S(1)} %bitcast.91), dimensions={0} | reverse | bytes 7077888 | tf_op jit(solution)/shard_map/rev | solution.py:106
  26.8 2.1 %collective-permute-start.6 = (bf16[2,3,2,4,256]{4,2,3,1,0:T(2,128)(2,1)S(1)}, bf16[2,3,2,4,256]{4,2,3,1,0:T(2,128)(2,1)S(1)}, u32[]{:S(2)}, u32[]{:S(2)}) collective-permute-start(bf16[2,3,2,4,256]{4,2,3,1,0:T(2,128)(2,1)S(1)} %broadcast_select_fusion.4), channel_id=1, source_target_pairs={{0,2},{1,3},{2,0},{3,1},{4,6},{5,7},{6,4},{7,5},{8,10},{9,11},{10,... | collective-permute-start | bytes 73736 | tf_op jit(solution)/shard_map/ppermute | solution.py:11
  30.9 2.8 %collective-permute-done.1 = bf16[2,3,2,4,256]{4,2,3,1,0:T(2,128)(2,1)S(1)} collective-permute-done((bf16[2,3,2,4,256]{4,2,3,1,0:T(2,128)(2,1)S(1)}, bf16[2,3,2,4,256]{4,2,3,1,0:T(2,128)(2,1)S(1)}, u32[]{:S(2)}, u32[]{:S(2)}) %collective-permute-start.1) | collective-permute-done | bytes 24608 | tf_op jit(solution)/shard_map/ppermute | solution.py:11
  33.9 1.1 maximum_maximum_fusion.2
  36.5 1.4 copy-done
  37.9 0.9 fusion.3
  38.7 1.4 collective-permute-start.2
  40.2 0.9 collective-permute-done.2
  41.1 1.0 fusion.15
  42.2 1.6 %collective-permute-start.3 = (bf16[1,3,2,4,256]{4,2,3,1,0:T(2,128)(2,1)S(1)}, bf16[1,3,2,4,256]{4,2,3,1,0:T(2,128)(2,1)S(1)}, u32[]{:S(2)}, u32[]{:S(2)}) collective-permute-start(bf16[1,3,2,4,256]{4,2,3,1,0:T(2,128)(2,1)S(1)} %maximum_bitcast_fusion.1), channel_id=1, source_target_pairs={{0,1},{1,0},{2,3},{3,2},{4,5},{5,4},{6,7},{7,6},{8,9},{9,8},{10,11... | collective-permute-start | bytes 36872 | tf_op jit(solution)/shard_map/ppermute | solution.py:11
  43.7 2.2 %collective-permute-done.3 = bf16[1,3,2,4,256]{4,2,3,1,0:T(2,128)(2,1)S(1)} collective-permute-done((bf16[1,3,2,4,256]{4,2,3,1,0:T(2,128)(2,1)S(1)}, bf16[1,3,2,4,256]{4,2,3,1,0:T(2,128)(2,1)S(1)}, u32[]{:S(2)}, u32[]{:S(2)}) %collective-permute-start.3) | collective-permute-done | bytes 12320 | tf_op jit(solution)/shard_map/ppermute | solution.py:11
  46.1 1.3 collective-permute-start.7
  47.4 2.5 %collective-permute-done.4 = bf16[2,3,2,4,256]{4,2,3,1,0:T(2,128)(2,1)S(1)} collective-permute-done((bf16[2,3,2,4,256]{4,2,3,1,0:T(2,128)(2,1)S(1)}, bf16[2,3,2,4,256]{4,2,3,1,0:T(2,128)(2,1)S(1)}, u32[]{:S(2)}, u32[]{:S(2)}) %collective-permute-start.4) | collective-permute-done | bytes 24608 | tf_op jit(solution)/shard_map/ppermute | solution.py:11
  52.0 1.4 copy-done.1
  53.4 0.9 fusion.6
  54.9 60.5 %all-gather.3.cloned.1.call-done = bf16[4992,256]{1,0:T(8,128)(2,1)} async-done(((bf16[312,256]{1,0:T(8,128)(2,1)}), bf16[4992,256]{1,0:T(8,128)(2,1)}) %all-gather.3.cloned.1.call-update) | async-done | bytes 2555920 | tf_op jit(solution)/shard_map/all_gather | solution.py:57
  115.4 2.5 %slice.389 = bf16[16,168,256]{2,1,0:T(8,128)(2,1)} slice(bf16[16,312,256]{2,1,0:T(8,128)(2,1)} %bitcast.93), slice={[0:16], [0:168], [0:256]} | slice | bytes 2752512 | tf_op jit(solution)/shard_map/slice | solution.py:59
  117.9 1.3 slice.391
  119.3 2.9 %reshape.170 = bf16[16,3,14,4,256]{4,3,2,1,0:T(4,128)(2,1)S(1)} reshape(bf16[16,168,256]{2,1,0:T(8,128)(2,1)} %slice.389) | data formatting | bytes 2752512 | tf_op jit(solution)/shard_map/reshape | solution.py:59
  122.2 3.5 %pad_dynamic-slice_fusion = (bf16[16,5,12,4,256]{4,3,2,1,0:T(4,128)(2,1)S(1)}, bf16[16,5,12,4,256]{4,3,2,1,0:T(4,128)(2,1)S(1)}) fusion(s32[]{:T(128)S(6)} %select_n.263, s32[]{:T(128)S(6)} %select_n.265, bf16[16,3,14,4,256]{4,3,2,1,0:T(4,128)(2,1)S(1)} %reshape.170, s32[]{:T(128)S(6)} %select_n.259, s32[]{:T(128)S(6)} %select_n.261), kind=kLoop, calls=%fused_computation | loop fusion | bytes 5308432 | tf_op jit(solution)/shard_map/dynamic_slice | solution.py:69
  125.7 3.8 %fusion = bf16[16,5,12,4,144]{4,3,2,1,0:T(4,128)(2,1)S(1)} fusion(s32[]{:T(128)S(6)} %select_n.266, bf16[16,5,12,4,256]{4,3,2,1,0:T(4,128)(2,1)S(1)} %get-tuple-element.12, bf16[16,5,12,4,256]{4,3,2,1,0:T(4,128)(2,1)S(1)} %get-tuple-element.11), kind=kLoop, calls=%fused_computation.4 | loop fusion | flops 2211840 | bytes 5038084 | tf_op jit(solution)/shard_map/concatenate | solution.py:75
  129.5 2.1 %fusion.30 = (bf16[16,3,12,4,144]{4,3,2,1,0:T(4,128)(2,1)}, bf16[16,3,12,4,144]{4,3,2,1,0:T(4,128)(2,1)S(1)}, bf16[16,3,12,4,144]{4,3,2,1,0:T(4,128)(2,1)S(1)}) fusion(bf16[16,5,12,4,144]{4,3,2,1,0:T(4,128)(2,1)S(1)} %fusion), kind=kLoop, calls=%fused_computation.210 | loop fusion | bytes 3981312 | tf_op jit(solution)/shard_map/slice | solution.py:81
  131.6 3.2 %reshape.171 = bf16[2304,144]{1,0:T(8,128)(2,1)} reshape(bf16[16,3,12,4,144]{4,3,2,1,0:T(4,128)(2,1)} %get-tuple-element.8) | data formatting | bytes 1327104 | tf_op jit(solution)/shard_map/reshape | solution.py:81
  134.7 1.7 %convolution_bitcast_fusion.2 = f32[1,1,144,256]{3,2,1,0:T(8,128)S(1)} fusion(bf16[2304,144]{1,0:T(8,128)(2,1)} %reshape.171, bf16[2304,256]{1,0:T(8,128)(2,1)S(1)} %bitcast.86), kind=kOutput, calls=%fused_computation.11 | convolution fusion | flops 169869312 | bytes 1990656 | tf_op jit(solution)/shard_map/dot_general | solution.py:80
  137.3 1.6 %reshape.173 = bf16[2304,144]{1,0:T(8,128)(2,1)} reshape(bf16[16,3,12,4,144]{4,3,2,1,0:T(4,128)(2,1)S(1)} %get-tuple-element.9) | data formatting | bytes 1327104 | tf_op jit(solution)/shard_map/reshape | solution.py:81
  138.8 1.7 %convolution_bitcast_fusion.1 = f32[1,1,144,256]{3,2,1,0:T(8,128)S(1)} fusion(bf16[2304,144]{1,0:T(8,128)(2,1)} %reshape.173, bf16[2304,256]{1,0:T(8,128)(2,1)S(1)} %bitcast.87), kind=kOutput, calls=%fused_computation.10 | convolution fusion | flops 169869312 | bytes 1990656 | tf_op jit(solution)/shard_map/dot_general | solution.py:80
  143.5 1.1 broadcast_in_dim.60
  (145 shorter events, 12.5 us)
Async XLA Ops:
  7.2 108.2 %all-gather.3.cloned.1.call-start = ((), (), s32[]{:S(2)}) async-start(), calls=%async_computation | async-start | bytes 2715648 | tf_op jit(solution)/shard_map/all_gather | solution.py:57
  9.6 0.6 copy-start.5
  10.3 15.7 %collective-permute-start.5 = (bf16[1,3,2,4,256]{4,2,3,1,0:T(2,128)(2,1)S(1)}, bf16[1,3,2,4,256]{4,2,3,1,0:T(2,128)(2,1)}, u32[]{:S(2)}, u32[]{:S(2)}) collective-permute-start(bf16[1,3,2,4,256]{4,2,3,1,0:T(2,128)(2,1)S(1)} %maximum_bitcast_fusion.2), channel_id=1, source_target_pairs={{0,1},{1,0},{2,3},{3,2},{4,5},{5,4},{6,7},{7,6},{8,9},{9,8},{10,11... | collective-permute-start | bytes 36872 | tf_op jit(solution)/shard_map/ppermute | solution.py:11
  14.3 0.6 copy-start.6
  15.6 13.3 %collective-permute-start = (bf16[1,3,2,4,256]{4,2,3,1,0:T(2,128)(2,1)}, bf16[1,3,2,4,256]{4,2,3,1,0:T(2,128)(2,1)}, u32[]{:S(2)}, u32[]{:S(2)}) collective-permute-start(bf16[1,3,2,4,256]{4,2,3,1,0:T(2,128)(2,1)} %maximum_bitcast_fusion), channel_id=1, source_target_pairs={{0,1},{1,0},{2,3},{3,2},{4,5},{5,4},{6,7},{7,6},{8,9},{9,8},{10,11... | collective-permute-start | bytes 36872 | tf_op jit(solution)/shard_map/ppermute | solution.py:11
  26.8 3.9 %collective-permute-start.6 = (bf16[2,3,2,4,256]{4,2,3,1,0:T(2,128)(2,1)S(1)}, bf16[2,3,2,4,256]{4,2,3,1,0:T(2,128)(2,1)S(1)}, u32[]{:S(2)}, u32[]{:S(2)}) collective-permute-start(bf16[2,3,2,4,256]{4,2,3,1,0:T(2,128)(2,1)S(1)} %broadcast_select_fusion.4), channel_id=1, source_target_pairs={{0,2},{1,3},{2,0},{3,1},{4,6},{5,7},{6,4},{7,5},{8,10},{9,11},{10,... | collective-permute-start | bytes 73736 | tf_op jit(solution)/shard_map/ppermute | solution.py:11
  29.8 3.9 %collective-permute-start.1 = (bf16[2,3,2,4,256]{4,2,3,1,0:T(2,128)(2,1)S(1)}, bf16[2,3,2,4,256]{4,2,3,1,0:T(2,128)(2,1)S(1)}, u32[]{:S(2)}, u32[]{:S(2)}) collective-permute-start(bf16[2,3,2,4,256]{4,2,3,1,0:T(2,128)(2,1)S(1)} %broadcast_select_fusion.6), channel_id=1, source_target_pairs={{0,2},{1,3},{2,0},{3,1},{4,6},{5,7},{6,4},{7,5},{8,10},{9,11},{10,... | collective-permute-start | bytes 73736 | tf_op jit(solution)/shard_map/ppermute | solution.py:11
  35.8 2.0 %copy-start = (bf16[1,27,256,256]{3,2,1,0:T(8,128)(2,1)S(1)}, bf16[1,27,256,256]{3,2,1,0:T(8,128)(2,1)}, u32[]{:S(2)}) copy-start(bf16[1,27,256,256]{3,2,1,0:T(8,128)(2,1)} %param.8) | copy-start | bytes 10616836
  35.9 2.0 %copy-start.8 = (bf16[1,1,3,12,4,256]{5,4,3,2,1,0:T(4,128)(2,1)S(1)}, bf16[1,1,3,12,4,256]{5,4,3,2,1,0:T(4,128)(2,1)}, u32[]{:S(2)}) copy-start(bf16[1,1,3,12,4,256]{5,4,3,2,1,0:T(4,128)(2,1)} %param.6) | copy-start | bytes 221188
  37.9 3.3 %copy-start.2 = (bf16[27,256,256]{1,2,0:T(8,128)(2,1)S(1)}, bf16[27,256,256]{1,2,0:T(8,128)(2,1)}, u32[]{:S(2)}) copy-start(bf16[27,256,256]{1,2,0:T(8,128)(2,1)} %rev.3) | copy-start | bytes 10616836
  37.9 3.3 %copy-start.7 = (bf16[1,1,3,12,4,256]{5,4,3,2,1,0:T(4,128)(2,1)S(1)}, bf16[1,1,3,12,4,256]{5,4,3,2,1,0:T(4,128)(2,1)}, u32[]{:S(2)}) copy-start(bf16[1,1,3,12,4,256]{5,4,3,2,1,0:T(4,128)(2,1)} %param.7) | copy-start | bytes 221188
  38.7 2.4 %collective-permute-start.2 = (bf16[3,12,4,256]{3,1,2,0:T(8,128)(2,1)S(1)}, bf16[3,12,4,256]{3,1,2,0:T(8,128)(2,1)S(1)}, u32[]{:S(2)}, u32[]{:S(2)}) collective-permute-start(bf16[3,12,4,256]{3,1,2,0:T(8,128)(2,1)S(1)} %fusion.3), channel_id=1, source_target_pairs={{0,16},{1,17},{2,18},{3,19},{4,20},{5,21},{6,22},{7,23},{8,24},{9,... | collective-permute-start | bytes 221192 | tf_op jit(solution)/shard_map/ppermute | solution.py:22
  42.2 3.8 %collective-permute-start.3 = (bf16[1,3,2,4,256]{4,2,3,1,0:T(2,128)(2,1)S(1)}, bf16[1,3,2,4,256]{4,2,3,1,0:T(2,128)(2,1)S(1)}, u32[]{:S(2)}, u32[]{:S(2)}) collective-permute-start(bf16[1,3,2,4,256]{4,2,3,1,0:T(2,128)(2,1)S(1)} %maximum_bitcast_fusion.1), channel_id=1, source_target_pairs={{0,1},{1,0},{2,3},{3,2},{4,5},{5,4},{6,7},{7,6},{8,9},{9,8},{10,11... | collective-permute-start | bytes 36872 | tf_op jit(solution)/shard_map/ppermute | solution.py:11
  46.0 3.9 %collective-permute-start.4 = (bf16[2,3,2,4,256]{4,2,3,1,0:T(2,128)(2,1)S(1)}, bf16[2,3,2,4,256]{4,2,3,1,0:T(2,128)(2,1)S(1)}, u32[]{:S(2)}, u32[]{:S(2)}) collective-permute-start(bf16[2,3,2,4,256]{4,2,3,1,0:T(2,128)(2,1)S(1)} %broadcast_select_fusion.5), channel_id=1, source_target_pairs={{0,2},{1,3},{2,0},{3,1},{4,6},{5,7},{6,4},{7,5},{8,10},{9,11},{10,... | collective-permute-start | bytes 73736 | tf_op jit(solution)/shard_map/ppermute | solution.py:11
  46.1 4.3 %collective-permute-start.7 = (bf16[3,12,4,256]{3,1,2,0:T(8,128)(2,1)S(1)}, bf16[3,12,4,256]{3,1,2,0:T(8,128)(2,1)S(1)}, u32[]{:S(2)}, u32[]{:S(2)}) collective-permute-start(bf16[3,12,4,256]{3,1,2,0:T(8,128)(2,1)S(1)} %get-tuple-element.13), channel_id=1, source_target_pairs={{16,0},{17,1},{18,2},{19,3},{20,4},{21,5},{22,6},{23,7},{24,8},{25... | collective-permute-start | bytes 221192 | tf_op jit(solution)/shard_map/ppermute | solution.py:22
  51.4 2.0 %copy-start.1 = (bf16[1,27,256,256]{3,2,1,0:T(8,128)(2,1)S(1)}, bf16[1,27,256,256]{3,2,1,0:T(8,128)(2,1)}, u32[]{:S(2)}) copy-start(bf16[1,27,256,256]{3,2,1,0:T(8,128)(2,1)} %param.8) | copy-start | bytes 10616836
  142.1 0.9 copy-start.3
  142.1 1.0 copy-start.4
Sparse Core Ops, SparseCore 0:
  51.3 64.0 all-gather.2
